TPU v7x, 32 devices: a whole 2x2x4 slice. The times are simulated.
32 devices in a mesh: head: 2 (over x), ffn: 4 (over y, core), row: 4 (over z).
Axes of the slice: x: 2, y: 2, z: 4, core: 2. Of those that a mesh axis runs over, the one named last changes fastest.
Arguments:
- inputs: bfloat16 [16, 640, 1024], P(('ffn', 'row'), 'head'), may hold values from -6 to 6
- first_values: bfloat16 [16, 640, 1024], P(('ffn', 'row'), 'head'), may hold values from -6 to 6
- lengths: int32 [16], P(('ffn', 'row')), may hold values from 512 to 640, as said below
- gain_attn: float32 [1024], replicated, may hold values from 0.5 to 1.5
- w_qkv: bfloat16 [1024, 3072], replicated, may hold values from -0.1875 to 0.1875
- w_out: bfloat16 [1024, 1024], replicated, may hold values from -3 to 3
- gain_mlp: float32 [1024], replicated, may hold values from 0.5 to 1.5
- w_gate: bfloat16 [1024, 2816], P(None, 'ffn'), may hold values from -0.1875 to 0.1875
- w_up: bfloat16 [1024, 2816], P(None, 'ffn'), may hold values from -0.1875 to 0.1875
- w_down: bfloat16 [2816, 1024], P('ffn'), may hold values from -0.109375 to 0.109375
- cotangent: bfloat16 [16, 640, 1024], P(('ffn', 'row'), 'head'), may hold values from -6 to 6
Outputs:
- output: bfloat16 [16, 640, 1024], P(('ffn', 'row'), 'head')
- grad_inputs: float32 [16, 640, 1024], P(('ffn', 'row'), 'head')
- grad_first_values: bfloat16 [16, 640, 1024], P(('ffn', 'row'), 'head')
- grad_gain_attn: float32 [1024], replicated
- grad_w_qkv: float32 [1024, 3072], P(('ffn', 'row'), 'head')
- grad_w_out: float32 [1024, 1024], P('head', ('ffn', 'row'))
- grad_gain_mlp: float32 [1024], replicated
- grad_w_gate: float32 [1024, 2816], P(('head', 'row'), 'ffn')
- grad_w_up: float32 [1024, 2816], P(('head', 'row'), 'ffn')
- grad_w_down: float32 [2816, 1024], P('ffn', ('head', 'row'))
Inputs may be any that keep to these rules, and one draw needn't show every extreme that they name: `lengths`: one bucket in every draw is full.
All inputs are finite; a program needn't handle non-finite values.
Results may differ from a plain program's by a relative error of at most 0.02.
Values may be sent and summed in bfloat16 or wider, within the bound.
No kernel may reach another device: no remote copies, remote signals or barrier semaphores. Data moves between devices by JAX's collectives and lax.ppermute only.
A program may use at most 128 MiB of HBM per device.

v0:
```python
import jax
import jax.numpy as jnp
from jax import lax
from jax.sharding import PartitionSpec as P

HEADS = 16
HD = 64
eps = 1e-06


def rms_scale(values):
    return lax.rsqrt(jnp.mean(values * values, axis=-1, keepdims=True) + eps)


def inner_rows(left, right):
    return lax.dot_general(
        left, right, (((0,), (0,)), ((), ())), preferred_element_type=jnp.float32
    )


def against(left, right):
    return lax.dot_general(
        left, right, (((1,), (1,)), ((), ())), preferred_element_type=jnp.float32
    )


def rotary(length, head_size):
    half_size = head_size // 2
    inverse = jnp.exp(
        -jnp.log(10000.0) * jnp.arange(half_size, dtype=jnp.float32) * 2.0 / head_size
    )
    angles = jnp.arange(length, dtype=jnp.float32)[:, None] * inverse[None, :]
    return (jnp.cos(angles), jnp.sin(angles))


def rotate(vectors, cosine, sine, sign):
    half_size = vectors.shape[-1] // 2
    first_half = vectors[..., :half_size]
    second_half = vectors[..., half_size:]
    cos_rows = cosine[:, None, :]
    sin_rows = sign * sine[:, None, :]
    return jnp.concatenate(
        [
            first_half * cos_rows - second_half * sin_rows,
            second_half * cos_rows + first_half * sin_rows,
        ],
        axis=-1,
    )


def masked_scores(q_rows, keys, start, valid):
    block_rows = q_rows.shape[0]
    raw = jnp.einsum("qhe,khe->hqk", q_rows, keys, preferred_element_type=jnp.float32)
    columns = jnp.arange(keys.shape[0], dtype=jnp.int32)
    positions = start + jnp.arange(block_rows, dtype=jnp.int32)
    allowed = (columns[None, :] <= positions[:, None]) & (columns[None, :] < valid)
    return jnp.where(allowed[None], 0.125 * raw, -1e30)


def attend_forward(query, keys, mixed, valid, block_rows):
    count = query.shape[0] // block_rows

    def step(carry, index):
        start = index * block_rows
        q_rows = lax.dynamic_slice_in_dim(query, start, block_rows, 0)
        scores = masked_scores(q_rows, keys, start, valid)
        top = jnp.max(scores, axis=-1, keepdims=True)
        expo = jnp.exp(scores - top)
        total = jnp.sum(expo, axis=-1, keepdims=True)
        weights = expo / total
        result = jnp.einsum(
            "hqk,khe->qhe", weights.astype(jnp.bfloat16), mixed, preferred_element_type=jnp.float32
        )
        return (carry, (result.astype(jnp.bfloat16), top + jnp.log(total)))

    _, (outs, log_sums) = lax.scan(step, 0, jnp.arange(count, dtype=jnp.int32))
    return (outs.reshape(query.shape), log_sums)


def attend_backward(query, keys, mixed, valid, log_sums, grad_out, block_rows):
    count = query.shape[0] // block_rows
    zeros = jnp.zeros(keys.shape, jnp.float32)

    def step(carry, index):
        key_sum, value_sum = carry
        start = index * block_rows
        q_rows = lax.dynamic_slice_in_dim(query, start, block_rows, 0)
        g_rows = lax.dynamic_slice_in_dim(grad_out, start, block_rows, 0)
        scores = masked_scores(q_rows, keys, start, valid)
        weights = jnp.exp(scores - log_sums[index])
        grad_w = jnp.einsum("qhe,khe->hqk", g_rows, mixed, preferred_element_type=jnp.float32)
        delta = jnp.sum(weights * grad_w, axis=-1, keepdims=True)
        grad_s = (weights * (grad_w - delta)).astype(jnp.bfloat16)
        grad_q = 0.125 * jnp.einsum(
            "hqk,khe->qhe", grad_s, keys, preferred_element_type=jnp.float32
        )
        key_sum = key_sum + 0.125 * jnp.einsum(
            "hqk,qhe->khe", grad_s, q_rows, preferred_element_type=jnp.float32
        )
        value_sum = value_sum + jnp.einsum(
            "hqk,qhe->khe", weights.astype(jnp.bfloat16), g_rows, preferred_element_type=jnp.float32
        )
        return ((key_sum, value_sum), grad_q)

    (grad_keys, grad_mixed), grad_query = lax.scan(
        step, (zeros, zeros), jnp.arange(count, dtype=jnp.int32)
    )
    return (grad_query.reshape(query.shape), grad_keys, grad_mixed)


def on_device(
    inputs,
    first_values,
    lengths,
    gain_attn,
    w_qkv,
    w_out,
    gain_mlp,
    w_gate,
    w_up,
    w_down,
    cotangent,
):
    tok_rows = inputs.shape[1]
    groups = lax.axis_size("head")
    heads_here = HEADS // groups
    span_rows = tok_rows * groups
    block_rows = span_rows // max(1, span_rows // 512)
    head_pos = lax.axis_index("head")
    valid_len = lengths[0]
    packed_cols = heads_here * 3 * HD
    out_cols = heads_here * HD
    rows_in = inputs[0].astype(jnp.float32)
    scale_one = rms_scale(rows_in)
    normed = (rows_in * scale_one * gain_attn).astype(jnp.bfloat16)
    earlier = first_values[0]
    w_heads = lax.dynamic_slice_in_dim(w_qkv, head_pos * packed_cols, packed_cols, 1)
    out_heads = lax.dynamic_slice_in_dim(w_out, head_pos * out_cols, out_cols, 0)
    gathered = lax.all_gather(normed, "head", axis=0, tiled=True)
    packed = jnp.dot(gathered, w_heads, preferred_element_type=jnp.float32).astype(jnp.bfloat16)
    early = lax.all_to_all(earlier, "head", split_axis=1, concat_axis=0, tiled=True)
    packed = packed.reshape(span_rows, heads_here, 3, HD)
    cosine, sine = rotary(span_rows, HD)
    query = rotate(packed[:, :, 0].astype(jnp.float32), cosine, sine, 1.0).astype(jnp.bfloat16)
    keys = rotate(packed[:, :, 1].astype(jnp.float32), cosine, sine, 1.0).astype(jnp.bfloat16)
    early_heads = early.reshape(span_rows, heads_here, HD).astype(jnp.float32)
    mixed = (0.5 * (packed[:, :, 2].astype(jnp.float32) + early_heads)).astype(jnp.bfloat16)
    attended, log_sums = attend_forward(query, keys, mixed, valid_len, block_rows)
    attended_flat = attended.reshape(span_rows, out_cols)
    piece = attended_flat
    projected = lax.psum_scatter(
        jnp.dot(piece, out_heads, preferred_element_type=jnp.float32),
        "head",
        scatter_dimension=0,
        tiled=True,
    )
    hidden = rows_in + projected
    scale_two = rms_scale(hidden)
    normed_two = (hidden * scale_two * gain_mlp).astype(jnp.bfloat16)
    mlp_rows = lax.all_gather(normed_two, "ffn", axis=0, tiled=True)
    gate_rows = jnp.dot(mlp_rows, w_gate, preferred_element_type=jnp.float32)
    up_rows = jnp.dot(mlp_rows, w_up, preferred_element_type=jnp.float32)
    sigmoid_gate = jax.nn.sigmoid(gate_rows)
    silu_gate = gate_rows * sigmoid_gate
    active = (silu_gate * up_rows).astype(jnp.bfloat16)
    piece = active
    down_rows = lax.psum_scatter(
        jnp.dot(piece, w_down, preferred_element_type=jnp.float32).astype(jnp.bfloat16),
        "ffn",
        scatter_dimension=0,
        tiled=True,
    ).astype(jnp.float32)
    output = (hidden + down_rows).astype(jnp.bfloat16)[None]
    grad_y = cotangent[0].astype(jnp.float32)
    grad_rows = lax.all_gather(grad_y.astype(jnp.bfloat16), "ffn", axis=0, tiled=True)
    grad_active = against(grad_rows, w_down)
    down_part = inner_rows(active, grad_rows)
    grad_gate = (
        grad_active * up_rows * sigmoid_gate * (1.0 + gate_rows * (1.0 - sigmoid_gate))
    ).astype(jnp.bfloat16)
    grad_up = (grad_active * silu_gate).astype(jnp.bfloat16)
    gate_part = inner_rows(mlp_rows, grad_gate)
    up_part = inner_rows(mlp_rows, grad_up)
    grad_normed_two = lax.psum_scatter(
        (against(grad_gate, w_gate) + against(grad_up, w_up)).astype(jnp.bfloat16),
        "ffn",
        scatter_dimension=0,
        tiled=True,
    ).astype(jnp.float32)
    grad_gain_two = jnp.sum(grad_normed_two * hidden * scale_two, axis=0)
    weighted_two = grad_normed_two * gain_mlp
    cube_two = scale_two * scale_two * scale_two
    grad_hidden = (
        grad_y
        + scale_two * weighted_two
        - hidden * cube_two * jnp.mean(weighted_two * hidden, axis=-1, keepdims=True)
    )
    grad_proj = grad_hidden.astype(jnp.bfloat16)
    proj_rows = lax.all_gather(grad_proj, "head", axis=0, tiled=True)
    grad_att = against(proj_rows, out_heads).astype(jnp.bfloat16)
    wout_heads = inner_rows(attended_flat, proj_rows)
    grad_att = grad_att.reshape(span_rows, heads_here, HD)
    grad_query, grad_keys, grad_mixed = attend_backward(
        query, keys, mixed, valid_len, log_sums, grad_att, block_rows
    )
    grad_packed = jnp.stack(
        [
            rotate(grad_query, cosine, sine, -1.0),
            rotate(grad_keys, cosine, sine, -1.0),
            0.5 * grad_mixed,
        ],
        axis=2,
    )
    grad_packed = grad_packed.astype(jnp.bfloat16).reshape(span_rows, packed_cols)
    grad_early = (0.5 * grad_mixed).astype(jnp.bfloat16).reshape(span_rows, out_cols)
    piece = grad_packed
    grad_normed = lax.psum_scatter(
        against(piece, w_heads).astype(jnp.bfloat16), "head", scatter_dimension=0, tiled=True
    ).astype(jnp.float32)
    wqkv_heads = inner_rows(gathered, grad_packed)
    grad_first = lax.all_to_all(grad_early, "head", split_axis=0, concat_axis=1, tiled=True)
    grad_gain_one = jnp.sum(grad_normed * rows_in * scale_one, axis=0)
    weighted_one = grad_normed * gain_attn
    cube_one = scale_one * scale_one * scale_one
    grad_in = (
        grad_hidden
        + scale_one * weighted_one
        - rows_in * cube_one * jnp.mean(weighted_one * rows_in, axis=-1, keepdims=True)
    )
    sum_qkv, sum_out = (
        lax.psum_scatter(
            wqkv_heads.astype(jnp.bfloat16), ("ffn", "row"), scatter_dimension=0, tiled=True
        ).astype(jnp.float32),
        lax.psum_scatter(
            wout_heads.astype(jnp.bfloat16), ("ffn", "row"), scatter_dimension=1, tiled=True
        ).astype(jnp.float32),
    )
    sum_gate, sum_up, sum_down = (
        lax.psum_scatter(gate_part, ("head", "row"), scatter_dimension=0, tiled=True),
        lax.psum_scatter(up_part, ("head", "row"), scatter_dimension=0, tiled=True),
        lax.psum_scatter(down_part, ("head", "row"), scatter_dimension=1, tiled=True),
    )
    gains_one, gains_two = lax.psum((grad_gain_one, grad_gain_two), ("head", "ffn", "row"))
    return (
        output,
        grad_in[None],
        grad_first[None],
        gains_one,
        sum_qkv,
        sum_out,
        gains_two,
        sum_gate,
        sum_up,
        sum_down,
    )


def solution(mesh):
    in_specs = (
        P(("ffn", "row"), "head", None),
        P(("ffn", "row"), "head", None),
        P(("ffn", "row")),
        P(),
        P(),
        P(),
        P(),
        P(None, "ffn"),
        P(None, "ffn"),
        P("ffn", None),
        P(("ffn", "row"), "head", None),
    )
    out_specs = (
        P(("ffn", "row"), "head", None),
        P(("ffn", "row"), "head", None),
        P(("ffn", "row"), "head", None),
        P(),
        P(("ffn", "row"), "head"),
        P("head", ("ffn", "row")),
        P(),
        P(("head", "row"), "ffn"),
        P(("head", "row"), "ffn"),
        P("ffn", ("head", "row")),
    )
    return jax.shard_map(
        on_device, mesh=mesh, in_specs=in_specs, out_specs=out_specs, check_vma=False
    )
```

profile of v0, /device:TPU:0, one launch (start us, length us, event | category | flops | bytes accessed | tf_op | source)
XLA Modules:
  0.0 695.1 jit_solution(10302706006738696550)
XLA Ops:
  13.5 4.3 all-to-all-start
  20.5 12.6 %all-to-all-done = bf16[320,2,512]{2,0,1:T(8,128)(2,1)} async-done(((bf16[320,2,512]{2,0,1:T(8,128)(2,1)}), bf16[320,2,512]{2,0,1:T(8,128)(2,1)}, u32[]{:S(2)}, u32[]{:S(2)}) %all-to-all-start) | async-done | bytes 655392 | tf_op jit(solution)/shard_map/all_to_all | solution.py:141
  42.9 5.8 convolution_convert_fusion.2
  48.7 4.0 copy.60
  62.5 4.0 fusion.29
  69.7 38.2 %reduce-scatter.10.cloned.1.call-done = f32[320,1024]{1,0:T(8,128)} async-done(((f32[640,1024]{1,0:T(8,128)}), f32[320,1024]{1,0:T(8,128)}) %reduce-scatter.10.cloned.1.call-update) | async-done | bytes 1310736 | tf_op jit(solution)/shard_map/reduce_scatter | solution.py:151
  111.6 24.9 %all-gather.8.cloned.1.call-done = bf16[1280,1024]{1,0:T(8,128)(2,1)} async-done(((bf16[320,1024]{1,0:T(8,128)(2,1)}), bf16[1280,1024]{1,0:T(8,128)(2,1)}) %all-gather.8.cloned.1.call-update) | async-done | bytes 2621456 | tf_op jit(solution)/shard_map/all_gather | solution.py:160
  136.5 6.1 fusion.68
  142.7 3.8 fusion.67
  146.5 17.1 %all-gather.12.cloned.1.call-done = bf16[1,1280,1024]{2,1,0:T(8,128)(2,1)} async-done(((bf16[1,320,1024]{2,1,0:T(8,128)(2,1)}), bf16[1,1280,1024]{2,1,0:T(8,128)(2,1)}) %all-gather.12.cloned.1.call-update) | async-done | bytes 2621456 | tf_op jit(solution)/shard_map/all_gather | solution.py:175
  163.6 8.8 %multiply_convert_fusion.1 = (bf16[1280,704]{0,1:T(8,128)(2,1)S(1)}, bf16[1280,704]{0,1:T(8,128)(2,1)S(1)}, bf16[1280,704]{0,1:T(8,128)(2,1)}) fusion(f32[1280,704]{0,1:T(8,128)} %fusion.67, f32[1280,704]{0,1:T(8,128)} %fusion.68, bf16[704,1024]{1,0:T(8,128)(2,1)} %param.20, bf16[1,1280,1024]{2,1,0:T(8,128)(2,1)} %all-gather.12.cloned.1.call-done), kind=kOutput, calls=%fused_computation.14 | convolution fusion | flops 1859010560 | bytes 16678912 | tf_op jit(solution)/shard_map/dot_general | solution.py:22
  174.9 3.9 add_convert_fusion
  178.8 34.8 %reduce-scatter.14.cloned.1.call-done = bf16[320,1024]{1,0:T(8,128)(2,1)} async-done(((bf16[1280,1024]{1,0:T(8,128)(2,1)}), bf16[320,1024]{1,0:T(8,128)(2,1)}) %reduce-scatter.14.cloned.1.call-update) | async-done | bytes 655376 | tf_op jit(solution)/shard_map/reduce_scatter | solution.py:184
  217.4 24.1 %all-gather.10.cloned.1.call-done = bf16[640,1024]{1,0:T(8,128)(2,1)} async-done(((bf16[320,1024]{1,0:T(8,128)(2,1)}), bf16[640,1024]{1,0:T(8,128)(2,1)}) %all-gather.10.cloned.1.call-update) | async-done | bytes 1310736 | tf_op jit(solution)/shard_map/all_gather | solution.py:199
  244.0 12.6 %multiply_reduce_fusion = (f32[8,640]{1,0:T(8,128)S(1)}, f32[8,640,640]{1,2,0:T(8,128)}) fusion(f32[8,640,640]{1,2,0:T(8,128)} %copy-done.2, f32[8,640]{1,0:T(8,128)S(1)} %log_add_fusion, bf16[640,8,64]{0,2,1:T(8,128)(2,1)S(1)} %bitcast.112, f32[640,8,64]{0,2,1:T(8,128)S(1)} %copy-done.8, bf16[640,8,3,64]{0,3,2,1:T(8,128)(2,1)} %bitcast.108), kind=kOutput, calls=%fused_computation.1 | convolution fusion | flops 430566400 | bytes 28876800 | tf_op jit(solution)/shard_map/while/body/eval_jaxpr/qhe,khe->hqk/dot_general | solution.py:91
  256.6 6.6 multiply_convert_fusion
  263.3 3.3 fusion.24
  273.1 7.1 %fusion.26 = bf16[8,64,640]{2,1,0:T(8,128)(2,1)S(1)} fusion(bf16[640,8,64]{0,2,1:T(8,128)(2,1)S(1)} %bitcast.113, f32[8,640,640]{1,2,0:T(8,128)} %copy-done.2, f32[8,640]{1,0:T(8,128)S(1)} %log_add_fusion), kind=kOutput, calls=%fused_computation.49 | convolution fusion | flops 426639360 | bytes 14438400 | tf_op jit(solution)/shard_map/while/body/eval_jaxpr/hqk,qhe->khe/dot_general | solution.py:100
  282.5 5.4 fusion.15
  288.0 5.2 convolution_convert_fusion.1
  294.8 5.4 convolution_convert_fusion
  301.7 5.4 fusion.10
  308.6 5.4 fusion.71
  315.5 5.3 fusion.70
  323.9 12.2 %all_to_all.29 = bf16[2,320,512]{2,1,0:T(8,128)(2,1)S(1)} all-to-all(bf16[2,320,512]{2,1,0:T(8,128)(2,1)S(1)} %copy.70), channel_id=1, replica_groups=mesh['head'=2,'ffn'=4,'row'=4] {'head'}, dimensions={0} | all-to-all | bytes 1310720 | tf_op jit(solution)/shard_map/all_to_all | solution.py:221
  339.5 13.2 %reduce-scatter.16.cloned.1.call-done = bf16[320,1024]{1,0:T(8,128)(2,1)} async-done(((bf16[640,1024]{1,0:T(8,128)(2,1)}), bf16[320,1024]{1,0:T(8,128)(2,1)}) %reduce-scatter.16.cloned.1.call-update) | async-done | bytes 655376 | tf_op jit(solution)/shard_map/reduce_scatter | solution.py:217
  354.3 39.6 %all-reduce = (f32[1024]{0:T(1024)}, f32[1024]{0:T(1024)}) all-reduce(f32[1024]{0:T(1024)S(1)} %get-tuple-element.53, f32[1024]{0:T(1024)S(1)} %copy-done.37), channel_id=1, replica_groups=mesh['head'=2,'ffn'=4,'row'=4] {'head','ffn','row'}, use_global_device_ids=true, to_apply=%region_12.13 | all-reduce | flops 2048 | bytes 16384 | tf_op jit(solution)/shard_map/psum | solution.py:243
  394.0 4.1 fusion.32
  398.0 62.5 %reduce-scatter.18.cloned.1.call-done = bf16[64,1536]{1,0:T(8,128)(2,1)} async-done(((bf16[1024,1536]{1,0:T(8,128)(2,1)}), bf16[64,1536]{1,0:T(8,128)(2,1)}) %reduce-scatter.18.cloned.1.call-update) | async-done | bytes 196624 | tf_op jit(solution)/shard_map/reduce_scatter | solution.py:231
  462.2 74.0 %reduce-scatter.26.cloned.1.call-done = f32[704,128]{1,0:T(8,128)} async-done(((f32[704,1024]{1,0:T(8,128)}), f32[704,128]{1,0:T(8,128)}) %reduce-scatter.26.cloned.1.call-update) | async-done | bytes 360464 | tf_op jit(solution)/shard_map/reduce_scatter | solution.py:241
  536.3 75.9 %reduce-scatter.24.cloned.1.call-done = f32[128,704]{0,1:T(8,128)} async-done(((f32[1024,704]{0,1:T(8,128)}), f32[128,704]{0,1:T(8,128)}) %reduce-scatter.24.cloned.1.call-update) | async-done | bytes 360464 | tf_op jit(solution)/shard_map/reduce_scatter | solution.py:240
  612.1 76.0 %reduce-scatter.22.cloned.1.call-done = f32[128,704]{0,1:T(8,128)} async-done(((f32[1024,704]{0,1:T(8,128)}), f32[128,704]{0,1:T(8,128)}) %reduce-scatter.22.cloned.1.call-update) | async-done | bytes 360464 | tf_op jit(solution)/shard_map/reduce_scatter | solution.py:239
  (178 shorter events, 67.9 us)
Async XLA Ops:
  7.2 60.1 %copy-start = (bf16[1024,1024]{1,0:T(8,128)(2,1)S(1)}, bf16[1024,1024]{1,0:T(8,128)(2,1)}, u32[]{:S(2)}) copy-start(bf16[1024,1024]{1,0:T(8,128)(2,1)} %param.16) | copy-start | bytes 6291460
  7.2 35.7 %all-gather.6.cloned.1.call-start = ((), (), s32[]{:S(2)}) async-start(), calls=%async_computation.11 | async-start | bytes 1966080 | tf_op jit(solution)/shard_map/all_gather | solution.py:139
  13.5 19.6 %all-to-all-start = ((bf16[320,2,512]{2,0,1:T(8,128)(2,1)}), bf16[320,2,512]{2,0,1:T(8,128)(2,1)}, u32[]{:S(2)}, u32[]{:S(2)}) async-start(bf16[320,2,512]{2,0,1:T(8,128)(2,1)} %copy.61), calls=%async_computation | async-start | bytes 1310720 | tf_op jit(solution)/shard_map/all_to_all | solution.py:141
  17.8 90.2 %reduce-scatter.10.cloned.1.call-start = ((), (), s32[]{:S(2)}) async-start(), calls=%async_computation.12 | async-start | bytes 3932160 | tf_op jit(solution)/shard_map/reduce_scatter | solution.py:151
  69.6 40.1 %copy-start.27 = (f32[1024]{0:T(1024)S(1)}, f32[1024]{0:T(1024)}, u32[]{:S(2)}) copy-start(f32[1024]{0:T(1024)} %param.17) | copy-start | bytes 12292
  69.7 66.8 %all-gather.8.cloned.1.call-start = ((), (), s32[]{:S(2)}) async-start(), calls=%async_computation.13 | async-start | bytes 3276800 | tf_op jit(solution)/shard_map/all_gather | solution.py:160
  109.7 106.1 %copy-start.28 = (f32[320]{0:T(512)}, f32[320]{0:T(512)S(1)}, u32[]{:S(2)}) copy-start(f32[320]{0:T(512)S(1)} %get-tuple-element.91) | copy-start | bytes 3844
  109.7 106.1 %copy-start.33 = (f32[320]{0:T(512)}, f32[320]{0:T(512)S(1)}, u32[]{:S(2)}) copy-start(f32[320]{0:T(512)S(1)} %get-tuple-element.90) | copy-start | bytes 3844
  110.8 52.8 %all-gather.12.cloned.1.call-start = ((), (), s32[]{:S(2)}) async-start(), calls=%async_computation.23 | async-start | bytes 3276800 | tf_op jit(solution)/shard_map/all_gather | solution.py:175
  111.3 102.2 %reduce-scatter.14.cloned.1.call-start = ((), (), s32[]{:S(2)}) async-start(), calls=%async_computation.15 | async-start | bytes 3276800 | tf_op jit(solution)/shard_map/reduce_scatter | solution.py:184
  178.8 62.7 %all-gather.10.cloned.1.call-start = ((), (), s32[]{:S(2)}) async-start(), calls=%async_computation.16 | async-start | bytes 1966080 | tf_op jit(solution)/shard_map/all_gather | solution.py:199
  217.1 120.9 %reduce-scatter.20.cloned.1.call-start = ((), (), s32[]{:S(2)}) async-start(), calls=%async_computation.19 | async-start | bytes 1114112 | tf_op jit(solution)/shard_map/reduce_scatter | solution.py:234
  243.9 12.6 %copy-start.9 = (bf16[640,512]{0,1:T(8,128)(2,1)}, bf16[640,512]{0,1:T(8,128)(2,1)S(1)}, u32[]{:S(2)}) copy-start(bf16[640,512]{0,1:T(8,128)(2,1)S(1)} %convolution_convert_fusion.4) | copy-start | bytes 1966084
  243.9 12.6 %slice-start = ((s8[13107200]{0:T(1024)(128)(4,1)}), s8[4194304]{0:T(1024)(128)(4,1)S(1)}, s32[]{:S(2)}) async-start(s8[13107200]{0:T(1024)(128)(4,1)} %bitcast.104), calls=%async_computation.24 | async-start | bytes 8388608
  244.0 12.6 %slice-start.1 = ((s8[13107200]{0:T(1024)(128)(4,1)}), s8[4194304]{0:T(1024)(128)(4,1)S(1)}, s32[]{:S(2)}) async-start(s8[13107200]{0:T(1024)(128)(4,1)} %bitcast.104), calls=%async_computation.25 | async-start | bytes 8388608
  244.0 12.6 %slice-start.2 = ((s8[13107200]{0:T(1024)(128)(4,1)}), s8[4194304]{0:T(1024)(128)(4,1)S(1)}, s32[]{:S(2)}) async-start(s8[13107200]{0:T(1024)(128)(4,1)} %bitcast.104), calls=%async_computation.26 | async-start | bytes 8388608
  244.0 12.6 %slice-start.3 = ((s8[13107200]{0:T(1024)(128)(4,1)}), s8[524288]{0:T(1024)(128)(4,1)S(1)}, s32[]{:S(2)}) async-start(s8[13107200]{0:T(1024)(128)(4,1)} %bitcast.104), calls=%async_computation.27 | async-start | bytes 1048576
  270.1 82.7 %reduce-scatter.16.cloned.1.call-start = ((), (), s32[]{:S(2)}) async-start(), calls=%async_computation.17 | async-start | bytes 1966080 | tf_op jit(solution)/shard_map/reduce_scatter | solution.py:217
  288.0 106.0 %reduce-scatter.12.cloned.1.call-start = ((), (), s32[]{:S(2)}) async-start(), calls=%async_computation.14 | async-start | bytes 3276800 | tf_op jit(solution)/shard_map/reduce_scatter | solution.py:167
  293.3 167.3 %reduce-scatter.18.cloned.1.call-start = ((), (), s32[]{:S(2)}) async-start(), calls=%async_computation.18 | async-start | bytes 3342336 | tf_op jit(solution)/shard_map/reduce_scatter | solution.py:231
  300.2 236.0 %reduce-scatter.26.cloned.1.call-start = ((), (), s32[]{:S(2)}) async-start(), calls=%async_computation.22 | async-start | bytes 3244032 | tf_op jit(solution)/shard_map/reduce_scatter | solution.py:241
  307.1 305.0 %reduce-scatter.24.cloned.1.call-start = ((), (), s32[]{:S(2)}) async-start(), calls=%async_computation.21 | async-start | bytes 3244032 | tf_op jit(solution)/shard_map/reduce_scatter | solution.py:240
  314.1 374.0 %reduce-scatter.22.cloned.1.call-start = ((), (), s32[]{:S(2)}) async-start(), calls=%async_computation.20 | async-start | bytes 3244032 | tf_op jit(solution)/shard_map/reduce_scatter | solution.py:239
  323.8 28.9 %copy-start.3 = (bf16[1,320,1024]{2,1,0:T(8,128)(2,1)S(1)}, bf16[1,320,1024]{2,1,0:T(8,128)(2,1)}, u32[]{:S(2)}) copy-start(bf16[1,320,1024]{2,1,0:T(8,128)(2,1)} %param.11) | copy-start | bytes 1966084
  323.8 28.9 %copy-start.30 = (f32[1024]{0:T(1024)S(1)}, f32[1024]{0:T(1024)}, u32[]{:S(2)}) copy-start(f32[1024]{0:T(1024)} %param.14) | copy-start | bytes 12292
  323.8 28.9 %copy-start.32 = (f32[320]{0:T(512)S(1)}, f32[320]{0:T(512)}, u32[]{:S(2)}) copy-start(f32[320]{0:T(512)} %copy-done.31) | copy-start | bytes 3844
  336.0 18.3 %copy-start.37 = (f32[1024]{0:T(1024)S(1)}, f32[1024]{0:T(1024)}, u32[]{:S(2)}) copy-start(f32[1024]{0:T(1024)} %get-tuple-element.51) | copy-start | bytes 12292
  336.0 57.9 %copy-start.29 = (f32[320]{0:T(512)S(1)}, f32[320]{0:T(512)}, u32[]{:S(2)}) copy-start(f32[320]{0:T(512)} %copy-done.28) | copy-start | bytes 3844
  336.0 57.9 %copy-start.34 = (f32[320]{0:T(512)S(1)}, f32[320]{0:T(512)}, u32[]{:S(2)}) copy-start(f32[320]{0:T(512)} %copy-done.33) | copy-start | bytes 3844
  336.0 57.9 %copy-start.36 = (f32[320]{0:T(512)S(1)}, f32[320]{0:T(512)}, u32[]{:S(2)}) copy-start(f32[320]{0:T(512)} %copy-done.35) | copy-start | bytes 3844
  336.0 57.9 %copy-start.38 = (f32[320]{0:T(512)S(1)}, f32[320]{0:T(512)}, u32[]{:S(2)}) copy-start(f32[320]{0:T(512)} %get-tuple-element.88) | copy-start | bytes 3844
  394.0 294.1 %copy-start.1 = (bf16[1024,1024]{1,0:T(8,128)(2,1)S(1)}, bf16[1024,1024]{1,0:T(8,128)(2,1)}, u32[]{:S(2)}) copy-start(bf16[1024,1024]{1,0:T(8,128)(2,1)} %param.16) | copy-start | bytes 6291460
  (36 other events, 102.5 us)
Sparse Core Ops, SparseCore 0:
  12.2 30.6 all-gather.5
  69.8 38.1 reduce-scatter.9
  110.9 25.5 all-gather.7
  138.0 25.5 all-gather.11
  178.9 34.6 reduce-scatter.13
  217.2 24.2 all-gather.9
  270.2 57.4 reduce-scatter.19
  330.6 22.1 reduce-scatter.15
  355.3 34.8 reduce-scatter.11
  394.3 66.1 reduce-scatter.17
  465.1 71.1 reduce-scatter.25
  540.7 71.4 reduce-scatter.23
  616.7 71.3 reduce-scatter.21
where the time goes:
time: 706 us; the launch traced here: 695 us
  waiting for transfers between devices  457 us (65%)
  matrix products  100 us (14%)
  blocking collectives  51.8 us (7%)
  other arithmetic  34.9 us (5%)
  local copies, waits for them, and re-layouts  29.6 us (4%)
  between operations  15.7 us (2%)
    reduce_scatter x1, waiting for transfers between devices, on_device(): lax.psum_scatter(gate_part, ('head', 'row'), scatter_dimension=0, tiled=T...  76 us
    reduce_scatter x1, waiting for transfers between devices, on_device(): lax.psum_scatter(up_part, ('head', 'row'), scatter_dimension=0, tiled=True)  75.9 us
    reduce_scatter x1, waiting for transfers between devices, on_device(): lax.psum_scatter(down_part, ('head', 'row'), scatter_dimension=1, tiled=T...  74 us
    reduce_scatter x1, waiting for transfers between devices, on_device(): lax.psum_scatter(wqkv_heads.astype(jnp.bfloat16), ('ffn', 'row'), scatter...  62.5 us
    psum x1, blocking collectives, on_device(): lax.psum((grad_gain_one, grad_gain_two), ('head', 'ffn', 'row'))  39.6 us
    reduce_scatter x1, waiting for transfers between devices, on_device(): lax.psum_scatter(jnp.dot(piece, out_heads, preferred_element_type=jnp.flo...  38.2 us
    reduce_scatter x1, waiting for transfers between devices, on_device(): lax.psum_scatter((against(grad_gate, w_gate) + against(grad_up, w_up)).as...  34.8 us
    all_gather x1, waiting for transfers between devices, on_device(): mlp_rows = lax.all_gather(normed_two, 'ffn', axis=0, tiled=True)  24.9 us
  transfers between devices with their start and end apart: 14, of which 12 were waited for; matrix products, arithmetic and copies ran while one was open for 11% of the time, Pallas kernels for 0%

commit v1 on v0

--- a/solution.py
+++ b/solution.py
@@ -6,6 +6,19 @@
 HEADS = 16
 HD = 64
 eps = 1e-06
+
+
+def collect(x, axis, dim):
+    ways = lax.axis_size(axis)
+    up = [(d, (d + 1) % ways) for d in range(ways)]
+    down = [(d, (d - 1) % ways) for d in range(ways)]
+    earlier, later = ([x], [x])
+    for _ in range(ways // 2):
+        earlier.append(lax.ppermute(earlier[-1], axis, up))
+    for _ in range((ways - 1) // 2):
+        later.append(lax.ppermute(later[-1], axis, down))
+    line = jnp.concatenate([*earlier[::-1], *later[1:]], axis=dim)
+    return jnp.roll(line, (lax.axis_index(axis) - ways // 2) * x.shape[dim], axis=dim)
 
 
 def rms_scale(values):
@@ -172,7 +185,7 @@
     ).astype(jnp.float32)
     output = (hidden + down_rows).astype(jnp.bfloat16)[None]
     grad_y = cotangent[0].astype(jnp.float32)
-    grad_rows = lax.all_gather(grad_y.astype(jnp.bfloat16), "ffn", axis=0, tiled=True)
+    grad_rows = collect(grad_y.astype(jnp.bfloat16), "ffn", 0)
     grad_active = against(grad_rows, w_down)
     down_part = inner_rows(active, grad_rows)
     grad_gate = (

time: 706 us -> 710 us (level)
  local copies, waits for them, and re-layouts: 29.6 us -> 43.3 us
    ppermute x0 -> x3, waiting for transfers between devices: none -> 35 us  [the longest x2 35 us: collect(): earlier.append(lax.ppermute(earlier[-1], axis, up))]
    all_gather x1, waiting for transfers between devices: 24.9 us -> 0.01 us  [on_device(): mlp_rows = lax.all_gather(normed_two, 'ffn', axis=0, tiled=True)]
    all_gather x1 -> x0, waiting for transfers between devices: 17.1 us -> none  [on_device(): lax.all_gather(grad_y.astype(jnp.bfloat16), 'ffn', axis=0, tiled=True)]
    unnamed x108 -> x117, local copies, waits for them, and re-layouts: 14.9 us -> 26.7 us
  transfers between devices with their start and end apart: 14 -> 16, of which waited for: 12 -> 12; matrix products, arithmetic and copies ran while one was open for 11% -> 11% of each run, Pallas kernels for 0% -> 0%
where the time goes in v1:
time: 710 us; the launch traced here: 699 us
  waiting for transfers between devices  452 us (64%)
  matrix products  94.4 us (13%)
  blocking collectives  51.8 us (7%)
  local copies, waits for them, and re-layouts  43.3 us (6%)
  other arithmetic  34.9 us (5%)
  between operations  16 us (2%)
  starting transfers between devices  7.49 us (1%)
    reduce_scatter x1, waiting for transfers between devices, on_device(): lax.psum_scatter(up_part, ('head', 'row'), scatter_dimension=0, tiled=True)  76.1 us
    reduce_scatter x1, waiting for transfers between devices, on_device(): lax.psum_scatter(gate_part, ('head', 'row'), scatter_dimension=0, tiled=T...  76 us
    reduce_scatter x1, waiting for transfers between devices, on_device(): lax.psum_scatter(down_part, ('head', 'row'), scatter_dimension=1, tiled=T...  74 us
    reduce_scatter x1, waiting for transfers between devices, on_device(): lax.psum_scatter(wqkv_heads.astype(jnp.bfloat16), ('ffn', 'row'), scatter...  62.6 us
    psum x1, blocking collectives, on_device(): lax.psum((grad_gain_one, grad_gain_two), ('head', 'ffn', 'row'))  39.6 us
    reduce_scatter x1, waiting for transfers between devices, on_device(): lax.psum_scatter(jnp.dot(piece, out_heads, preferred_element_type=jnp.flo...  38.2 us
    reduce_scatter x1, waiting for transfers between devices, on_device(): lax.psum_scatter((against(grad_gate, w_gate) + against(grad_up, w_up)).as...  36.3 us
    ppermute x2, waiting for transfers between devices, collect(): earlier.append(lax.ppermute(earlier[-1], axis, up))  35 us
  transfers between devices with their start and end apart: 16, of which 12 were waited for; matrix products, arithmetic and copies ran while one was open for 11% of the time, Pallas kernels for 0%

profile of v1, /device:TPU:0, one launch (start us, length us, event | category | flops | bytes accessed | tf_op | source)
XLA Modules:
  0.0 699.5 jit_solution(9591232208006623306)
XLA Ops:
  13.5 4.3 all-to-all-start
  20.5 12.6 %all-to-all-done = bf16[320,2,512]{2,0,1:T(8,128)(2,1)} async-done(((bf16[320,2,512]{2,0,1:T(8,128)(2,1)}), bf16[320,2,512]{2,0,1:T(8,128)(2,1)}, u32[]{:S(2)}, u32[]{:S(2)}) %all-to-all-start) | async-done | bytes 655392 | tf_op jit(solution)/shard_map/all_to_all | solution.py:154
  39.7 3.2 all-gather.4.cloned.1.call-done
  42.9 5.8 convolution_convert_fusion.2
  48.7 4.0 copy.60
  62.4 4.0 fusion.29
  69.7 38.2 %reduce-scatter.10.cloned.1.call-done = f32[320,1024]{1,0:T(8,128)} async-done(((f32[640,1024]{1,0:T(8,128)}), f32[320,1024]{1,0:T(8,128)}) %reduce-scatter.10.cloned.1.call-update) | async-done | bytes 1310736 | tf_op jit(solution)/shard_map/reduce_scatter | solution.py:164
  110.8 10.4 %collective-permute-done = bf16[320,1024]{1,0:T(8,128)(2,1)} collective-permute-done((bf16[320,1024]{1,0:T(8,128)(2,1)}, bf16[320,1024]{1,0:T(8,128)(2,1)}, u32[]{:S(2)}, u32[]{:S(2)}) %collective-permute-start) | collective-permute-done | bytes 655392 | tf_op jit(solution)/shard_map/ppermute | solution.py:17
  123.2 24.6 %collective-permute-done.1 = bf16[320,1024]{1,0:T(8,128)(2,1)} collective-permute-done((bf16[320,1024]{1,0:T(8,128)(2,1)}, bf16[320,1024]{1,0:T(8,128)(2,1)}, u32[]{:S(2)}, u32[]{:S(2)}) %collective-permute-start.1) | collective-permute-done | bytes 655392 | tf_op jit(solution)/shard_map/ppermute | solution.py:17
  161.5 4.4 fusion.70
  168.0 6.6 multiply_convert_fusion.1
  177.0 3.9 add_convert_fusion
  181.0 36.3 %reduce-scatter.14.cloned.1.call-done = bf16[320,1024]{1,0:T(8,128)(2,1)} async-done(((bf16[1280,1024]{1,0:T(8,128)(2,1)}), bf16[320,1024]{1,0:T(8,128)(2,1)}) %reduce-scatter.14.cloned.1.call-update) | async-done | bytes 655376 | tf_op jit(solution)/shard_map/reduce_scatter | solution.py:197
  221.0 24.1 %all-gather.8.cloned.1.call-done = bf16[640,1024]{1,0:T(8,128)(2,1)} async-done(((bf16[320,1024]{1,0:T(8,128)(2,1)}), bf16[640,1024]{1,0:T(8,128)(2,1)}) %all-gather.8.cloned.1.call-update) | async-done | bytes 1310736 | tf_op jit(solution)/shard_map/all_gather | solution.py:212
  247.7 12.6 %multiply_reduce_fusion = (f32[8,640]{1,0:T(8,128)S(1)}, f32[8,640,640]{1,2,0:T(8,128)}) fusion(f32[8,640,640]{1,2,0:T(8,128)} %copy-done.2, f32[8,640]{1,0:T(8,128)S(1)} %log_add_fusion, bf16[640,8,64]{0,2,1:T(8,128)(2,1)S(1)} %bitcast.108, f32[640,8,64]{0,2,1:T(8,128)S(1)} %copy-done.9, bf16[640,8,3,64]{0,3,2,1:T(8,128)(2,1)} %bitcast.104), kind=kOutput, calls=%fused_computation.1 | convolution fusion | flops 430566400 | bytes 28876800 | tf_op jit(solution)/shard_map/while/body/eval_jaxpr/qhe,khe->hqk/dot_general | solution.py:104
  260.3 6.6 multiply_convert_fusion
  266.9 3.3 fusion.24
  276.8 7.1 %fusion.26 = bf16[8,64,640]{2,1,0:T(8,128)(2,1)S(1)} fusion(bf16[640,8,64]{0,2,1:T(8,128)(2,1)S(1)} %bitcast.109, f32[8,640,640]{1,2,0:T(8,128)} %copy-done.2, f32[8,640]{1,0:T(8,128)S(1)} %log_add_fusion), kind=kOutput, calls=%fused_computation.49 | convolution fusion | flops 426639360 | bytes 14438400 | tf_op jit(solution)/shard_map/while/body/eval_jaxpr/hqk,qhe->khe/dot_general | solution.py:113
  286.2 5.4 fusion.15
  291.7 5.2 convolution_convert_fusion.1
  298.5 5.4 convolution_convert_fusion
  305.3 5.4 fusion.10
  312.3 5.4 fusion.73
  319.2 5.3 fusion.72
  327.5 12.2 %all_to_all.29 = bf16[2,320,512]{2,1,0:T(8,128)(2,1)S(1)} all-to-all(bf16[2,320,512]{2,1,0:T(8,128)(2,1)S(1)} %copy.70), channel_id=1, replica_groups=mesh['head'=2,'ffn'=4,'row'=4] {'head'}, dimensions={0} | all-to-all | bytes 1310720 | tf_op jit(solution)/shard_map/all_to_all | solution.py:234
  343.2 13.2 %reduce-scatter.16.cloned.1.call-done = bf16[320,1024]{1,0:T(8,128)(2,1)} async-done(((bf16[640,1024]{1,0:T(8,128)(2,1)}), bf16[320,1024]{1,0:T(8,128)(2,1)}) %reduce-scatter.16.cloned.1.call-update) | async-done | bytes 655376 | tf_op jit(solution)/shard_map/reduce_scatter | solution.py:230
  358.0 39.6 %all-reduce = (f32[1024]{0:T(1024)}, f32[1024]{0:T(1024)}) all-reduce(f32[1024]{0:T(1024)S(1)} %get-tuple-element.53, f32[1024]{0:T(1024)S(1)} %copy-done.38), channel_id=1, replica_groups=mesh['head'=2,'ffn'=4,'row'=4] {'head','ffn','row'}, use_global_device_ids=true, to_apply=%region_12.13 | all-reduce | flops 2048 | bytes 16384 | tf_op jit(solution)/shard_map/psum | solution.py:256
  397.6 4.1 fusion.32
  401.7 62.6 %reduce-scatter.18.cloned.1.call-done = bf16[64,1536]{1,0:T(8,128)(2,1)} async-done(((bf16[1024,1536]{1,0:T(8,128)(2,1)}), bf16[64,1536]{1,0:T(8,128)(2,1)}) %reduce-scatter.18.cloned.1.call-update) | async-done | bytes 196624 | tf_op jit(solution)/shard_map/reduce_scatter | solution.py:244
  466.0 74.0 %reduce-scatter.26.cloned.1.call-done = f32[704,128]{1,0:T(8,128)} async-done(((f32[704,1024]{1,0:T(8,128)}), f32[704,128]{1,0:T(8,128)}) %reduce-scatter.26.cloned.1.call-update) | async-done | bytes 360464 | tf_op jit(solution)/shard_map/reduce_scatter | solution.py:254
  540.0 76.1 %reduce-scatter.24.cloned.1.call-done = f32[128,704]{0,1:T(8,128)} async-done(((f32[1024,704]{0,1:T(8,128)}), f32[128,704]{0,1:T(8,128)}) %reduce-scatter.24.cloned.1.call-update) | async-done | bytes 360464 | tf_op jit(solution)/shard_map/reduce_scatter | solution.py:253
  616.1 76.0 %reduce-scatter.22.cloned.1.call-done = f32[128,704]{0,1:T(8,128)} async-done(((f32[1024,704]{0,1:T(8,128)}), f32[128,704]{0,1:T(8,128)}) %reduce-scatter.22.cloned.1.call-update) | async-done | bytes 360464 | tf_op jit(solution)/shard_map/reduce_scatter | solution.py:252
  (191 shorter events, 81.7 us)
Async XLA Ops:
  7.2 60.0 %copy-start = (bf16[1024,1024]{1,0:T(8,128)(2,1)S(1)}, bf16[1024,1024]{1,0:T(8,128)(2,1)}, u32[]{:S(2)}) copy-start(bf16[1024,1024]{1,0:T(8,128)(2,1)} %param.16) | copy-start | bytes 6291460
  7.2 35.7 %all-gather.4.cloned.1.call-start = ((), (), s32[]{:S(2)}) async-start(), calls=%async_computation.11 | async-start | bytes 1966080 | tf_op jit(solution)/shard_map/all_gather | solution.py:152
  13.5 19.6 %all-to-all-start = ((bf16[320,2,512]{2,0,1:T(8,128)(2,1)}), bf16[320,2,512]{2,0,1:T(8,128)(2,1)}, u32[]{:S(2)}, u32[]{:S(2)}) async-start(bf16[320,2,512]{2,0,1:T(8,128)(2,1)} %copy.61), calls=%async_computation | async-start | bytes 1310720 | tf_op jit(solution)/shard_map/all_to_all | solution.py:154
  17.8 90.1 %reduce-scatter.10.cloned.1.call-start = ((), (), s32[]{:S(2)}) async-start(), calls=%async_computation.12 | async-start | bytes 3932160 | tf_op jit(solution)/shard_map/reduce_scatter | solution.py:164
  69.6 40.1 %copy-start.28 = (f32[1024]{0:T(1024)S(1)}, f32[1024]{0:T(1024)}, u32[]{:S(2)}) copy-start(f32[1024]{0:T(1024)} %param.17) | copy-start | bytes 12292
  69.6 91.9 %all-gather.6.cloned.1.call-start = ((), (), s32[]{:S(2)}) async-start(), calls=%async_computation.13 | async-start | bytes 3276800 | tf_op jit(solution)/shard_map/all_gather | solution.py:173
  109.7 109.8 %copy-start.29 = (f32[320]{0:T(512)}, f32[320]{0:T(512)S(1)}, u32[]{:S(2)}) copy-start(f32[320]{0:T(512)S(1)} %get-tuple-element.91) | copy-start | bytes 3844
  109.7 109.8 %copy-start.34 = (f32[320]{0:T(512)}, f32[320]{0:T(512)S(1)}, u32[]{:S(2)}) copy-start(f32[320]{0:T(512)S(1)} %get-tuple-element.90) | copy-start | bytes 3844
  110.7 106.5 %reduce-scatter.14.cloned.1.call-start = ((), (), s32[]{:S(2)}) async-start(), calls=%async_computation.15 | async-start | bytes 3276800 | tf_op jit(solution)/shard_map/reduce_scatter | solution.py:197
  110.8 10.5 %collective-permute-start = (bf16[320,1024]{1,0:T(8,128)(2,1)}, bf16[320,1024]{1,0:T(8,128)(2,1)}, u32[]{:S(2)}, u32[]{:S(2)}) collective-permute-start(bf16[320,1024]{1,0:T(8,128)(2,1)} %bitcast.100), channel_id=1, source_target_pairs={{0,4},{4,8},{8,12},{12,0},{1,5},{5,9},{9,13},{13,1},{2,6},{6,10},{... | collective-permute-start | bytes 1966088 | tf_op jit(solution)/shard_map/ppermute | solution.py:17
  121.3 26.5 %collective-permute-start.1 = (bf16[320,1024]{1,0:T(8,128)(2,1)}, bf16[320,1024]{1,0:T(8,128)(2,1)}, u32[]{:S(2)}, u32[]{:S(2)}) collective-permute-start(bf16[320,1024]{1,0:T(8,128)(2,1)} %collective-permute-done), channel_id=1, source_target_pairs={{0,4},{4,8},{8,12},{12,0},{1,5},{5,9},{9,13},{13,1},{2,6},{6,10},{... | collective-permute-start | bytes 1966088 | tf_op jit(solution)/shard_map/ppermute | solution.py:17
  122.8 29.8 %collective-permute-start.2 = (bf16[320,1024]{1,0:T(8,128)(2,1)}, bf16[320,1024]{1,0:T(8,128)(2,1)}, u32[]{:S(2)}, u32[]{:S(2)}) collective-permute-start(bf16[320,1024]{1,0:T(8,128)(2,1)} %bitcast.101), channel_id=1, source_target_pairs={{0,12},{4,0},{8,4},{12,8},{1,13},{5,1},{9,5},{13,9},{2,14},{6,2},{... | collective-permute-start | bytes 1966088 | tf_op jit(solution)/shard_map/ppermute | solution.py:19
  123.2 28.6 %copy-start.4 = (bf16[1,320,1024]{2,1,0:T(8,128)(2,1)S(1)}, bf16[1,320,1024]{2,1,0:T(8,128)(2,1)}, u32[]{:S(2)}) copy-start(bf16[1,320,1024]{2,1,0:T(8,128)(2,1)} %param.21) | copy-start | bytes 1966084
  180.9 64.2 %all-gather.8.cloned.1.call-start = ((), (), s32[]{:S(2)}) async-start(), calls=%async_computation.16 | async-start | bytes 1966080 | tf_op jit(solution)/shard_map/all_gather | solution.py:212
  220.7 121.0 %reduce-scatter.20.cloned.1.call-start = ((), (), s32[]{:S(2)}) async-start(), calls=%async_computation.19 | async-start | bytes 1114112 | tf_op jit(solution)/shard_map/reduce_scatter | solution.py:247
  247.6 12.6 %copy-start.10 = (bf16[640,512]{0,1:T(8,128)(2,1)}, bf16[640,512]{0,1:T(8,128)(2,1)S(1)}, u32[]{:S(2)}) copy-start(bf16[640,512]{0,1:T(8,128)(2,1)S(1)} %convolution_convert_fusion.4) | copy-start | bytes 1966084
  247.6 12.6 %slice-start = ((s8[13107200]{0:T(1024)(128)(4,1)}), s8[4194304]{0:T(1024)(128)(4,1)S(1)}, s32[]{:S(2)}) async-start(s8[13107200]{0:T(1024)(128)(4,1)} %bitcast.98), calls=%async_computation.23 | async-start | bytes 8388608
  273.8 82.7 %reduce-scatter.16.cloned.1.call-start = ((), (), s32[]{:S(2)}) async-start(), calls=%async_computation.17 | async-start | bytes 1966080 | tf_op jit(solution)/shard_map/reduce_scatter | solution.py:230
  291.6 106.0 %reduce-scatter.12.cloned.1.call-start = ((), (), s32[]{:S(2)}) async-start(), calls=%async_computation.14 | async-start | bytes 3276800 | tf_op jit(solution)/shard_map/reduce_scatter | solution.py:180
  296.9 167.4 %reduce-scatter.18.cloned.1.call-start = ((), (), s32[]{:S(2)}) async-start(), calls=%async_computation.18 | async-start | bytes 3342336 | tf_op jit(solution)/shard_map/reduce_scatter | solution.py:244
  303.9 236.2 %reduce-scatter.26.cloned.1.call-start = ((), (), s32[]{:S(2)}) async-start(), calls=%async_computation.22 | async-start | bytes 3244032 | tf_op jit(solution)/shard_map/reduce_scatter | solution.py:254
  310.8 305.3 %reduce-scatter.24.cloned.1.call-start = ((), (), s32[]{:S(2)}) async-start(), calls=%async_computation.21 | async-start | bytes 3244032 | tf_op jit(solution)/shard_map/reduce_scatter | solution.py:253
  317.7 374.4 %reduce-scatter.22.cloned.1.call-start = ((), (), s32[]{:S(2)}) async-start(), calls=%async_computation.20 | async-start | bytes 3244032 | tf_op jit(solution)/shard_map/reduce_scatter | solution.py:252
  327.5 28.9 %copy-start.3 = (bf16[1,320,1024]{2,1,0:T(8,128)(2,1)S(1)}, bf16[1,320,1024]{2,1,0:T(8,128)(2,1)}, u32[]{:S(2)}) copy-start(bf16[1,320,1024]{2,1,0:T(8,128)(2,1)} %param.11) | copy-start | bytes 1966084
  327.5 28.9 %copy-start.31 = (f32[1024]{0:T(1024)S(1)}, f32[1024]{0:T(1024)}, u32[]{:S(2)}) copy-start(f32[1024]{0:T(1024)} %param.14) | copy-start | bytes 12292
  327.5 28.9 %copy-start.33 = (f32[320]{0:T(512)S(1)}, f32[320]{0:T(512)}, u32[]{:S(2)}) copy-start(f32[320]{0:T(512)} %copy-done.32) | copy-start | bytes 3844
  339.7 18.3 %copy-start.38 = (f32[1024]{0:T(1024)S(1)}, f32[1024]{0:T(1024)}, u32[]{:S(2)}) copy-start(f32[1024]{0:T(1024)} %get-tuple-element.51) | copy-start | bytes 12292
  339.7 57.9 %copy-start.30 = (f32[320]{0:T(512)S(1)}, f32[320]{0:T(512)}, u32[]{:S(2)}) copy-start(f32[320]{0:T(512)} %copy-done.29) | copy-start | bytes 3844
  339.7 57.9 %copy-start.35 = (f32[320]{0:T(512)S(1)}, f32[320]{0:T(512)}, u32[]{:S(2)}) copy-start(f32[320]{0:T(512)} %copy-done.34) | copy-start | bytes 3844
  339.7 57.9 %copy-start.37 = (f32[320]{0:T(512)S(1)}, f32[320]{0:T(512)}, u32[]{:S(2)}) copy-start(f32[320]{0:T(512)} %copy-done.36) | copy-start | bytes 3844
  339.7 57.9 %copy-start.39 = (f32[320]{0:T(512)S(1)}, f32[320]{0:T(512)}, u32[]{:S(2)}) copy-start(f32[320]{0:T(512)} %get-tuple-element.88) | copy-start | bytes 3844
  397.6 294.5 %copy-start.1 = (bf16[1024,1024]{1,0:T(8,128)(2,1)S(1)}, bf16[1024,1024]{1,0:T(8,128)(2,1)}, u32[]{:S(2)}) copy-start(bf16[1024,1024]{1,0:T(8,128)(2,1)} %param.16) | copy-start | bytes 6291460
  (39 other events, 129.9 us)
Sparse Core Ops, SparseCore 0:
  12.2 30.6 all-gather.3
  69.7 38.1 reduce-scatter.9
  110.8 34.9 all-gather.5
  181.0 36.1 reduce-scatter.13
  220.8 24.2 all-gather.7
  273.9 57.3 reduce-scatter.19
  334.2 22.1 reduce-scatter.15
  358.9 34.8 reduce-scatter.11
  398.1 66.1 reduce-scatter.17
  468.7 71.2 reduce-scatter.25
  544.6 71.4 reduce-scatter.23
  620.5 71.5 reduce-scatter.21
